TPU v7x, 32 devices: a whole 2x2x4 slice. The times are simulated.
32 devices in a mesh: pair: 16 (over z, x, core), virt: 2 (over y).
Axes of the slice: x: 2, y: 2, z: 4, core: 2. Of those that a mesh axis runs over, the one named last changes fastest.
Arguments:
- amplitudes: bfloat16 [80, 512, 512], P('pair', 'virt'), may hold values from -6 to 6
- cycle_inter: bfloat16 [48, 512, 512], P('pair', 'virt'), may hold values from -0.5 to 0.5
- pair_orbitals: int32 [80, 2], P('pair'), may hold values from 0 to 47, as said below
- occ_irrep: int32 [48], replicated, may hold values from 0 to 7
- virt_irrep: int32 [512], replicated, may hold values from 0 to 7
Outputs:
- residual: bfloat16 [80, 512, 512], P('pair', 'virt')
Inputs may be any that keep to these rules, and one draw needn't show every extreme that they name: `pair_orbitals`: each row (i, j) has i < j, and no two rows are equal.
All inputs are finite; a program needn't handle non-finite values.
Results may differ from a plain program's by a relative error of at most 0.001.
Values may be sent and summed in bfloat16 or wider, within the bound.
No kernel may reach another device: no remote copies, remote signals or barrier semaphores. Data moves between devices by JAX's collectives and lax.ppermute only.
A program may use at most 64 MiB of HBM per device.

v0:
```python
import jax
import jax.numpy as jnp
from jax import lax
from jax.sharding import PartitionSpec as P


def local(amplitudes, cycle_inter, pair_orbitals, occ_irrep, virt_irrep):
    slab = amplitudes.shape[1]
    row_start = lax.axis_index("virt") * slab
    local_irrep = lax.dynamic_slice_in_dim(virt_irrep, row_start, slab)
    first = pair_orbitals[:, 0]
    second = pair_orbitals[:, 1]
    orbital_ids = jnp.arange(occ_irrep.shape[0], dtype=jnp.int32)
    sym_first = jnp.sum(
        jnp.where(first[:, None] == orbital_ids[None, :], occ_irrep[None, :], 0), axis=1
    )
    sym_second = jnp.sum(
        jnp.where(second[:, None] == orbital_ids[None, :], occ_irrep[None, :], 0), axis=1
    )
    pair_sym = jnp.bitwise_xor(sym_first, sym_second)
    block_sym = jnp.bitwise_xor(local_irrep[:, None], virt_irrep[None, :])
    zero_bf = jnp.zeros((), jnp.bfloat16)
    masked_t = jnp.where(block_sym[None, :, :] == pair_sym[:, None, None], amplitudes, zero_bf)
    inter_mask = local_irrep[:, None] == virt_irrep[None, :]
    piece = lax.all_gather(cycle_inter, "pair", axis=0, tiled=True)
    ids = jnp.arange(piece.shape[0], dtype=jnp.int32)
    pick_second = (second[:, None] == ids[None, :]).astype(jnp.bfloat16)
    pick_first = (first[:, None] == ids[None, :]).astype(jnp.bfloat16)
    new_second = jnp.einsum("po,ocb->pcb", pick_second, piece, preferred_element_type=jnp.float32)
    new_first = jnp.einsum("po,ocb->pcb", pick_first, piece, preferred_element_type=jnp.float32)
    g_second = jnp.where(inter_mask[None], new_second, 0.0).astype(jnp.bfloat16)
    g_first = jnp.where(inter_mask[None], new_first, 0.0).astype(jnp.bfloat16)

    def mirror_rows(start, count):
        return jnp.einsum("pca,pcb->apb", g_first, masked_t, preferred_element_type=jnp.float32)

    terms = []
    terms.append(mirror_rows)
    t_columns = lax.all_to_all(masked_t, "virt", split_axis=2, concat_axis=1, tiled=True)

    def cycle_rows(start, count):
        return jnp.einsum("pac,pcb->apb", t_columns, g_second, preferred_element_type=jnp.float32)

    terms.append(cycle_rows)
    start = jnp.int32(0)
    result = terms[0](start, slab * lax.axis_size("virt"))
    for other in terms[1:]:
        result = result + other(start, slab * lax.axis_size("virt"))
    summed = lax.psum_scatter(result, "virt", scatter_dimension=0, tiled=True)
    total = summed.astype(jnp.bfloat16)
    return jnp.transpose(total, (1, 0, 2))


def solution(mesh):
    placed = (P("pair", "virt", None), P("pair", "virt", None), P("pair", None), P(), P())
    return jax.shard_map(
        local, mesh=mesh, in_specs=placed, out_specs=P("pair", "virt", None), check_vma=False
    )
```

profile of v0, /device:TPU:0, one launch (start us, length us, event | category | flops | bytes accessed | tf_op | source)
XLA Modules:
  0.0 212.9 jit_solution(15422062621394534236)
XLA Ops:
  6.5 0.0 all-gather.2.cloned.1.call-start
  6.5 0.7 all-gather.2.cloned.1.call-update
  7.3 0.8 dynamic_slice.3
  8.0 0.8 broadcast_xor_fusion
  8.8 0.0 copy-start.1
  8.8 0.0 copy-start.2
  8.8 0.2 copy.25
  9.0 3.2 %copy.26 = bf16[5,256,512]{1,0,2:T(8,128)(2,1)S(1)} copy(bf16[5,256,512]{2,1,0:T(8,128)(2,1)} %param.5) | data formatting | bytes 2621440 | tf_op args[0]
  12.2 0.0 copy-done.1
  12.2 0.0 copy-done.2
  12.3 0.2 select_reduce_fusion
  12.5 1.9 compare_select_fusion
  14.4 0.0 copy-start
  14.4 4.4 %all-to-all-start = ((bf16[5,256,512]{1,0,2:T(8,128)(2,1)}), bf16[5,256,512]{1,0,2:T(8,128)(2,1)S(1)}, u32[]{:S(2)}, u32[]{:S(2)}) async-start(bf16[5,256,512]{1,0,2:T(8,128)(2,1)} %compare_select_fusion), calls=%async_computation | async-start | bytes 4194304 | tf_op jit(solution)/shard_map/all_to_all | solution.py:39
  18.8 0.0 reduce-scatter.2.cloned.1.call-start
  18.8 0.0 copy-done
  18.8 0.1 broadcast_compare_fusion
  18.9 25.7 %all-to-all-done = bf16[5,256,512]{1,0,2:T(8,128)(2,1)S(1)} async-done(((bf16[5,256,512]{1,0,2:T(8,128)(2,1)}), bf16[5,256,512]{1,0,2:T(8,128)(2,1)S(1)}, u32[]{:S(2)}, u32[]{:S(2)}) %all-to-all-start) | async-done | bytes 1310752 | tf_op jit(solution)/shard_map/all_to_all | solution.py:39
  44.6 1.4 copy.32
  46.0 66.8 %all-gather.2.cloned.1.call-done = bf16[48,256,512]{2,1,0:T(8,128)(2,1)} async-done(((bf16[3,256,512]{2,1,0:T(8,128)(2,1)}), bf16[48,256,512]{2,1,0:T(8,128)(2,1)}) %all-gather.2.cloned.1.call-update) | async-done | bytes 12582928 | tf_op jit(solution)/shard_map/all_gather | solution.py:25
  112.8 0.0 slice-start
  112.8 11.5 %fusion.2 = bf16[5,256,512]{2,0,1:T(8,128)(2,1)S(1)} fusion(bf16[48,256,512]{2,1,0:T(8,128)(2,1)} %all-gather.2.cloned.1.call-done, s32[5]{0:T(128)S(1)} %get-tuple-element.8), kind=kOutput, calls=%fused_computation.2 | convolution fusion | flops 62914800 | bytes 13893652 | tf_op jit(solution)/shard_map/po,ocb->pcb/dot_general | solution.py:30
  124.3 3.1 %fusion.6 = f32[5,512,512]{2,1,0:T(8,128)S(1)} fusion(bf16[5,256,512]{2,0,1:T(8,128)(2,1)S(1)} %fusion.2, bf16[5,256,512]{1,0,2:T(8,128)(2,1)} %compare_select_fusion, pred[256,512]{1,0:T(8,128)(4,1)S(1)} %broadcast_compare_fusion), kind=kOutput, calls=%fused_computation.10 | convolution fusion | flops 671744000 | bytes 7995392 | tf_op jit(solution)/shard_map/pca,pcb->apb/dot_general | solution.py:35
  127.5 0.0 slice-done
  127.5 0.0 slice-done.1
  127.5 0.0 slice-done.2
  127.5 7.0 %fusion = bf16[5,256,512]{2,0,1:T(8,128)(2,1)S(1)} fusion(bf16[48,256,512]{2,1,0:T(8,128)(2,1)S(1)} %bitcast.20, s32[5]{0:T(128)S(1)} %get-tuple-element.7), kind=kOutput, calls=%fused_computation | convolution fusion | flops 62914800 | bytes 13893652 | tf_op jit(solution)/shard_map/po,ocb->pcb/dot_general | solution.py:29
  134.5 4.0 %add_bitcast_fusion = f32[512,5,512]{0,2,1:T(8,128)} fusion(f32[5,512,512]{2,1,0:T(8,128)S(1)} %fusion.6, bf16[5,512,256]{2,1,0:T(8,128)(2,1)S(1)} %bitcast.22, bf16[5,256,512]{2,0,1:T(8,128)(2,1)S(1)} %fusion, pred[256,512]{1,0:T(8,128)(4,1)S(1)} %broadcast_compare_fusion), kind=kOutput, calls=%fused_computation.4 | convolution fusion | flops 673054720 | bytes 13238272 | tf_op jit(solution)/shard_map/pac,pcb->apb/dot_general | solution.py:42
  138.4 0.0 reduce-scatter.2.cloned.1.call-update
  138.5 64.2 %reduce-scatter.2.cloned.1.call-done = f32[256,5,512]{0,2,1:T(8,128)} async-done(((f32[512,5,512]{0,2,1:T(8,128)}), f32[256,5,512]{0,2,1:T(8,128)}) %reduce-scatter.2.cloned.1.call-update) | async-done | bytes 2621456 | tf_op jit(solution)/shard_map/reduce_scatter | solution.py:49
  202.6 1.9 convert_bitcast_fusion
  204.5 1.6 copy.34
  (5 shorter events, 0.0 us)
Async XLA Ops:
  6.5 106.3 %all-gather.2.cloned.1.call-start = ((), (), s32[]{:S(2)}) async-start(), calls=%async_computation.2 | async-start | bytes 13369344 | tf_op jit(solution)/shard_map/all_gather | solution.py:25
  8.8 3.4 %copy-start.1 = (s32[5,2]{0,1:T(2,128)S(1)}, s32[5,2]{0,1:T(2,128)}, u32[]{:S(2)}) copy-start(s32[5,2]{0,1:T(2,128)} %param.7) | copy-start | bytes 124
  8.8 3.4 %copy-start.2 = (s32[48]{0:T(128)S(1)}, s32[48]{0:T(128)}, u32[]{:S(2)}) copy-start(s32[48]{0:T(128)} %param.8) | copy-start | bytes 580
  14.4 4.4 %copy-start = (s32[512]{0:T(512)S(1)}, s32[512]{0:T(512)}, u32[]{:S(2)}) copy-start(s32[512]{0:T(512)} %param.9) | copy-start | bytes 6148
  14.4 30.2 %all-to-all-start = ((bf16[5,256,512]{1,0,2:T(8,128)(2,1)}), bf16[5,256,512]{1,0,2:T(8,128)(2,1)S(1)}, u32[]{:S(2)}, u32[]{:S(2)}) async-start(bf16[5,256,512]{1,0,2:T(8,128)(2,1)} %compare_select_fusion), calls=%async_computation | async-start | bytes 4194304 | tf_op jit(solution)/shard_map/all_to_all | solution.py:39
  18.8 183.8 %reduce-scatter.2.cloned.1.call-start = ((), (), s32[]{:S(2)}) async-start(), calls=%async_computation.3 | async-start | bytes 7864320 | tf_op jit(solution)/shard_map/reduce_scatter | solution.py:49
  112.8 14.7 %slice-start = ((s8[12582912]{0:T(1024)(128)(4,1)}), s8[4194304]{0:T(1024)(128)(4,1)S(1)}, s32[]{:S(2)}) async-start(s8[12582912]{0:T(1024)(128)(4,1)} %bitcast.19), calls=%async_computation.4 | async-start | bytes 8388608
  112.8 14.7 %slice-start.1 = ((s8[12582912]{0:T(1024)(128)(4,1)}), s8[4194304]{0:T(1024)(128)(4,1)S(1)}, s32[]{:S(2)}) async-start(s8[12582912]{0:T(1024)(128)(4,1)} %bitcast.19), calls=%async_computation.5 | async-start | bytes 8388608
  124.3 3.2 %slice-start.2 = ((s8[12582912]{0:T(1024)(128)(4,1)}), s8[4194304]{0:T(1024)(128)(4,1)S(1)}, s32[]{:S(2)}) async-start(s8[12582912]{0:T(1024)(128)(4,1)} %bitcast.19), calls=%async_computation.6 | async-start | bytes 8388608
Sparse Core Ops, SparseCore 0:
  9.6 103.1 all-gather.1
  138.6 63.9 reduce-scatter.1
where the time goes:
time: 213 us
  waiting for transfers between devices  157 us (74%)
  matrix products  25.6 us (12%)
  between operations  13.5 us (6%)
  local copies, waits for them, and re-layouts  7.12 us (3%)
  other arithmetic  4.93 us (2%)
  starting transfers between devices  4.4 us (2%)
    all_gather x1, waiting for transfers between devices, local(): piece = lax.all_gather(cycle_inter, 'pair', axis=0, tiled=True)  66.8 us
    reduce_scatter x1, waiting for transfers between devices, local(): summed = lax.psum_scatter(result, 'virt', scatter_dimension=0, tiled=True)  64.2 us
    all_to_all x1, waiting for transfers between devices, local(): lax.all_to_all(masked_t, 'virt', split_axis=2, concat_axis=1, tiled=True)  25.7 us
    dot_general x1, matrix products, local(): jnp.einsum('po,ocb->pcb', pick_first, piece, preferred_element_type=jnp.f...  11.5 us
    dot_general x1, matrix products, local(): jnp.einsum('po,ocb->pcb', pick_second, piece, preferred_element_type=jnp....  6.98 us
    all_to_all x1, starting transfers between devices, local(): lax.all_to_all(masked_t, 'virt', split_axis=2, concat_axis=1, tiled=True)  4.39 us
  transfers between devices with their start and end apart: 3, of which 3 were waited for; matrix products, arithmetic and copies ran while one was open for 4% of the time, Pallas kernels for 0%

commit v1 on v0

v1 whole, which is shorter than its diff:
```python
import functools

import jax
import jax.numpy as jnp
import numpy as np
from jax import lax
from jax.experimental import pallas as pl
from jax.experimental.pallas import tpu as pltpu
from jax.sharding import PartitionSpec as P

IRREPS = 8
CAP = 96
F32 = jnp.float32
BF16 = jnp.bfloat16
ANY = pl.BlockSpec(memory_space=pl.ANY)
SMEM = pl.BlockSpec(memory_space=pltpu.SMEM)
VMEM = pl.BlockSpec(memory_space=pltpu.VMEM)


def dot(a, b, ca, cb):
    return lax.dot_general(a, b, (((ca,), (cb,)), ((), ())), preferred_element_type=F32)


def chip_ring(mesh):
    devices = list(mesh.devices[:, 0])
    count = len(devices)
    try:
        coords = [tuple(d.coords) for d in devices]
    except AttributeError:
        coords = [(i // 2,) for i in range(count)]
    chips = sorted(set(coords))
    varying = [a for a in range(len(chips[0])) if len({c[a] for c in chips}) > 1]
    order = None
    if len(varying) == 2:
        first = sorted({c[varying[0]] for c in chips})
        second = sorted({c[varying[1]] for c in chips})
        if len(first) % 2:
            first, second, varying = second, first, varying[::-1]
        if len(first) % 2 == 0 and len(first) * len(second) == len(chips):
            path = []
            for row, f in enumerate(first):
                inner = second[1:] if row % 2 == 0 else second[:0:-1]
                path += [(f, s) for s in inner]
            path += [(f, second[0]) for f in first[::-1]]
            order = {p: n for n, p in enumerate(path)}
    if order is None:
        position = {c: n for n, c in enumerate(chips)}
    else:
        position = {c: order[(c[varying[0]], c[varying[1]])] for c in chips}
    place, core, seen = [], [], {}
    for c in coords:
        place.append(position[c])
        core.append(seen.get(c, 0))
        seen[c] = core[-1] + 1
    return place, core


def one_hot_rows(irrep, symmetry=0):
    labels = lax.broadcasted_iota(jnp.int32, (IRREPS, irrep.shape[1]), 0)
    return (jnp.bitwise_xor(irrep, symmetry) == labels).astype(BF16)


def tables(irrep, start, slab, cap):
    size = irrep.shape[1]
    hot = one_hot_rows(irrep)
    below = lax.broadcasted_iota(jnp.int32, (size, size), 0) < lax.broadcasted_iota(
        jnp.int32, (size, size), 1
    )
    counted = dot(hot, below.astype(BF16), 1, 0)
    rank = jnp.sum(counted * hot.astype(F32), axis=0, keepdims=True).astype(jnp.int32)
    ranks = (lax.broadcasted_iota(jnp.int32, (cap, size), 0) == rank).astype(BF16)
    pick = (
        lax.broadcasted_iota(jnp.int32, (size, slab), 0)
        == lax.broadcasted_iota(jnp.int32, (size, slab), 1) + start
    ).astype(BF16)
    hot_own = dot(hot, pick, 1, 0).astype(BF16)
    ranks_own = dot(ranks, pick, 1, 0).astype(BF16)
    return hot, hot_own, ranks, ranks_own


def compact_inter_kernel(irrep_ref, inter_ref, out_ref, ranks_ref, ranks_own_ref, hot_own_ref):
    count, slab, size = inter_ref.shape
    cap = out_ref.shape[1]
    start = lax.axis_index("virt") * slab
    hot, hot_own, ranks, ranks_own = tables(irrep_ref[...], start, slab, cap)
    ranks_ref[...] = ranks
    ranks_own_ref[...] = ranks_own
    hot_own_ref[...] = hot_own
    mask = dot(hot_own, hot, 0, 0).astype(BF16)
    for k in range(count):
        out_ref[k] = dot(ranks, inter_ref[k] * mask, 1, 1).astype(BF16)


def pair_symmetry(orbitals_ref, occ_ref, p):
    return jnp.bitwise_xor(occ_ref[orbitals_ref[p, 0]], occ_ref[orbitals_ref[p, 1]])


def compact_amp_kernel(orbitals_ref, occ_ref, irrep_ref, hot_own_ref, ranks_ref, amp_ref, out_ref):
    symmetry = pair_symmetry(orbitals_ref, occ_ref, pl.program_id(0))
    mask = dot(hot_own_ref[...], one_hot_rows(irrep_ref[...], symmetry), 0, 0).astype(BF16)
    out_ref[0] = dot(ranks_ref[...], amp_ref[0] * mask, 1, 1).astype(BF16)


def residual_kernel(
    pieces,
    ring,
    owned,
    width,
    orbitals_ref,
    occ_ref,
    place_ref,
    core_ref,
    irrep_ref,
    hot_own_ref,
    ranks_ref,
    ranks_own_ref,
    amp_ref,
    *refs,
):
    flat = list(refs)
    inter_refs = [[flat.pop(0) for _ in range(n)] for n in pieces]
    amp_refs = [flat.pop(0) for _ in pieces]
    out_ref, inter, amps, inter_sem, amp_sem = flat
    p = pl.program_id(0)
    pairs = pl.num_programs(0)
    me = lax.axis_index("pair")
    virt = lax.axis_index("virt")
    parts = len(pieces)

    def lanes(piece):
        if parts == 1:
            return pl.ds(0, width)
        where = lax.rem(virt + piece, parts)
        return pl.ds(pl.multiple_of(where * width, width), width)

    def amp_copy(pair, piece):
        return pltpu.make_async_copy(
            amp_refs[piece].at[pair], amps.at[pair, :, lanes(piece)], amp_sem.at[pair, piece]
        )

    def inter_copy(source, row, slot, piece):
        return pltpu.make_async_copy(
            source.at[row], inter.at[slot, :, lanes(piece)], inter_sem.at[slot, piece]
        )

    @pl.when(p == 0)
    def _():
        @pl.loop(0, 2 * pairs)
        def _(slot):
            orbital = orbitals_ref[slot // 2, slot % 2]
            owner = orbital // owned
            row = orbital - owner * owned
            gap = lax.rem(place_ref[me] - place_ref[owner] + ring, ring)
            which = gap + ring * (core_ref[me] != core_ref[owner]).astype(jnp.int32)
            for piece, sources in enumerate(inter_refs):
                if len(sources) == 1:
                    inter_copy(sources[0], slot, slot, piece).start()
                    continue
                for n, source in enumerate(sources):

                    @pl.when(which == n)
                    def _(source=source, piece=piece):
                        inter_copy(source, row, slot, piece).start()

        @pl.loop(0, pairs)
        def _(pair):
            for piece in range(parts):
                amp_copy(pair, piece).start()

    hot = one_hot_rows(irrep_ref[...])
    symmetry = pair_symmetry(orbitals_ref, occ_ref, p)
    hot_own = hot_own_ref[...]
    mask = dot(hot_own, one_hot_rows(irrep_ref[...], symmetry), 0, 0)
    diagonal = dot(hot_own, hot, 0, 0)
    masked = amp_ref[0] * mask.astype(BF16)
    for piece in range(parts):
        amp_copy(p, piece).wait()
        for end in range(2):
            inter_copy(inter_refs[piece][0], 0, 2 * p + end, piece).wait()
    total = dot(masked, inter[2 * p + 1], 1, 1)
    mirror = (dot(ranks_own_ref[...], inter[2 * p], 0, 0) * diagonal).astype(BF16)
    total = total + dot(mirror, amps[p], 1, 1)
    spread = dot(total.astype(BF16), ranks_ref[...], 1, 0)
    out_ref[0] = (spread * mask).astype(BF16)


def blocked(cap, place, core, first_tables, amplitudes, inter_own, pair_orbitals, occ_irrep, irrep):
    ranks, ranks_own, hot_own = first_tables
    pairs, slab, size = amplitudes.shape
    owned = inter_own.shape[0]
    parts = lax.axis_size("virt")
    ring = len(place) // 2
    at = {(place[i], core[i]): i for i in range(len(place))}

    def hop(x, step):
        return lax.ppermute(
            x, "pair", [(i, at[(place[i] + step) % ring, core[i]]) for i in range(len(place))]
        )

    def swap(x):
        return lax.ppermute(x, "pair", [(i, at[place[i], 1 - core[i]]) for i in range(len(place))])

    def others(x):
        return [
            lax.ppermute(x, "virt", [((i + d) % parts, i) for i in range(parts)])
            for d in range(1, parts)
        ]

    def gathered(x, last):
        found = {0: x}
        ahead = behind = x
        for step in range(1, ring // 2):
            ahead, behind = hop(ahead, 1), hop(behind, -1)
            found[step], found[ring - step] = ahead, behind
        found[ring // 2] = hop(ahead if last > 0 else behind, last)
        mine = [found[d] for d in range(ring)]
        return mine + [swap(b) for b in mine]

    amps_own = pl.pallas_call(
        compact_amp_kernel,
        grid=(pairs,),
        in_specs=[SMEM, SMEM, VMEM, VMEM, VMEM, pl.BlockSpec((1, slab, size), lambda p: (p, 0, 0))],
        out_specs=pl.BlockSpec((1, cap, slab), lambda p: (p, 0, 0)),
        out_shape=jax.ShapeDtypeStruct((pairs, cap, slab), BF16),
        cost_estimate=pl.CostEstimate(
            flops=2 * pairs * cap * slab * size,
            bytes_accessed=2 * pairs * slab * (size + cap),
            transcendentals=0,
        ),
        name="compact_amp",
    )(pair_orbitals, occ_irrep, irrep, hot_own, ranks, amplitudes)

    amps_others = others(amps_own)
    width = slab
    if parts == 2 and slab % 128 == 0:
        inter_others = others(inter_own)
        inter_pieces = [gathered(inter_own, 1), gathered(inter_others[0], -1)]
        amp_pieces = [amps_own, amps_others[0]]
    else:
        width = slab * parts
        turn = jnp.remainder(jnp.arange(parts) - lax.axis_index("virt"), parts)

        def assembled(x, rest):
            whole = jnp.transpose(jnp.take(jnp.stack([x] + rest), turn, axis=0), (1, 2, 0, 3))
            return whole.reshape(x.shape[0], cap, width)

        every = lax.all_gather(inter_own, "pair", axis=0, tiled=True)
        chosen = jnp.take(every, pair_orbitals.reshape(-1), axis=0)
        inter_pieces = [[assembled(chosen, others(chosen))]]
        amp_pieces = [assembled(amps_own, amps_others)]

    operands = [b for piece in inter_pieces for b in piece] + amp_pieces
    kernel = functools.partial(
        residual_kernel, [len(piece) for piece in inter_pieces], ring, owned, width
    )
    row = pl.BlockSpec((1, slab, size), lambda p: (p, 0, 0))
    return pl.pallas_call(
        kernel,
        grid=(pairs,),
        in_specs=[SMEM] * 4 + [VMEM] * 4 + [row] + [ANY] * len(operands),
        out_specs=row,
        out_shape=jax.ShapeDtypeStruct((pairs, slab, size), BF16),
        scratch_shapes=[
            pltpu.VMEM((2 * pairs, cap, size), BF16),
            pltpu.VMEM((pairs, cap, size), BF16),
            pltpu.SemaphoreType.DMA((2 * pairs, len(inter_pieces))),
            pltpu.SemaphoreType.DMA((pairs, len(inter_pieces))),
        ],
        name="residual",
    )(
        pair_orbitals,
        occ_irrep,
        jnp.asarray(np.array(place, np.int32)),
        jnp.asarray(np.array(core, np.int32)),
        irrep,
        hot_own,
        ranks,
        ranks_own,
        amplitudes,
        *operands,
    )


def compact_inter(cap, cycle_inter, irrep):
    owned, slab, size = cycle_inter.shape
    return pl.pallas_call(
        compact_inter_kernel,
        in_specs=[VMEM, VMEM],
        out_specs=[VMEM] * 4,
        out_shape=[
            jax.ShapeDtypeStruct((owned, cap, slab), BF16),
            jax.ShapeDtypeStruct((cap, size), BF16),
            jax.ShapeDtypeStruct((cap, slab), BF16),
            jax.ShapeDtypeStruct((IRREPS, slab), BF16),
        ],
        name="compact_inter",
    )(irrep, cycle_inter)


def local(place, core, amplitudes, cycle_inter, pair_orbitals, occ_irrep, virt_irrep):
    size = amplitudes.shape[2]
    irrep = virt_irrep.reshape(1, size)
    labels = jnp.arange(IRREPS, dtype=jnp.int32)
    widest = jnp.max(jnp.sum((virt_irrep[None, :] == labels[:, None]).astype(jnp.int32), axis=1))

    def run(cap):
        inter_own, *first_tables = compact_inter(cap, cycle_inter, irrep)
        return blocked(
            cap, place, core, first_tables, amplitudes, inter_own, pair_orbitals, occ_irrep, irrep
        )

    cap = min(CAP, size)
    return lax.cond(widest <= cap, lambda: run(cap), lambda: run(size))


def solution(mesh):
    place, core = chip_ring(mesh)
    placed = (P("pair", "virt", None), P("pair", "virt", None), P("pair", None), P(), P())
    return jax.shard_map(
        functools.partial(local, place, core),
        mesh=mesh,
        in_specs=placed,
        out_specs=P("pair", "virt", None),
        check_vma=False,
    )
```

time: 213 us -> 58.9 us (0.28)
  waiting for transfers between devices: 157 us -> 13.9 us
  matrix products: 25.6 us -> 0 us
  starting transfers between devices: 4.4 us -> 23.1 us
  Pallas kernels: 0 us -> 16.8 us
  between operations: 13.5 us -> 0.66 us
  local copies, waits for them, and re-layouts: 7.12 us -> 2.22 us
  other arithmetic: 4.93 us -> 1.43 us
    all_gather x1 -> x0, waiting for transfers between devices: 66.8 us -> none  [local(): piece = lax.all_gather(cycle_inter, 'pair', axis=0, tiled=True)]
    reduce_scatter x1 -> x0, waiting for transfers between devices: 64.2 us -> none  [local(): summed = lax.psum_scatter(result, 'virt', scatter_dimension=0, tiled=True)]
    all_to_all x1 -> x0, waiting for transfers between devices: 25.7 us -> none  [local(): lax.all_to_all(masked_t, 'virt', split_axis=2, concat_axis=1, tiled=True)]
    dot_general x4 -> x0, matrix products: 25.6 us -> none  [the longest x1 11.5 us: local(): jnp.einsum('po,ocb->pcb', pick_first, piece, preferred_element_type=jnp.f...]
    ppermute x0 -> x32, starting transfers between devices: none -> 23.1 us  [the longest x14 19.2 us: hop(): lax.ppermute(x, 'pair', [(i, at[(place[i] + step) % ring, core[i]]) for i...]
    pallas_call x0 -> x3, Pallas kernels: none -> 16.8 us  [the longest x1 9.21 us: blocked(): pl.pallas_call(kernel, grid=(pairs,), in_specs=[SMEM] * 4 + [VMEM] * 4 +...]
    ppermute x0 -> x32, waiting for transfers between devices: none -> 13.9 us  [the longest x14 12.6 us: hop(): lax.ppermute(x, 'pair', [(i, at[(place[i] + step) % ring, core[i]]) for i...]
    all_to_all x1 -> x0, starting transfers between devices: 4.39 us -> none  [local(): lax.all_to_all(masked_t, 'virt', split_axis=2, concat_axis=1, tiled=True)]
  transfers between devices with their start and end apart: 3 -> 32, of which waited for: 3 -> 13; matrix products, arithmetic and copies ran while one was open for 4% -> 2% of each run, Pallas kernels for 0% -> 8%
where the time goes in v1:
time: 58.9 us; the launch traced here: 58.5 us
  starting transfers between devices  23.1 us (39%)
  Pallas kernels  16.8 us (29%)
  waiting for transfers between devices  13.9 us (24%)
  local copies, waits for them, and re-layouts  2.22 us (4%)
  other arithmetic  1.43 us (2%)
  between operations  0.66 us (1%)
    ppermute x14, starting transfers between devices, hop(): lax.ppermute(x, 'pair', [(i, at[(place[i] + step) % ring, core[i]]) for i...  19.2 us
    ppermute x14, waiting for transfers between devices, hop(): lax.ppermute(x, 'pair', [(i, at[(place[i] + step) % ring, core[i]]) for i...  12.6 us
    pallas_call x1, Pallas kernels, blocked(): pl.pallas_call(kernel, grid=(pairs,), in_specs=[SMEM] * 4 + [VMEM] * 4 +...  9.21 us
    pallas_call x1, Pallas kernels, blocked(): pl.pallas_call(compact_amp_kernel, grid=(pairs,), in_specs=[SMEM, SMEM, V...  4.81 us
    ppermute x2, starting transfers between devices, others(): lax.ppermute(x, 'virt', [((i + d) % parts, i) for i in range(parts)])  3.09 us
    pallas_call x1, Pallas kernels, compact_inter(): pl.pallas_call(compact_inter_kernel, in_specs=[VMEM, VMEM], out_specs=[VM...  2.74 us
    another operation x1, local copies, waits for them, and re-layouts  1.35 us
    ppermute x16, waiting for transfers between devices, swap(): lax.ppermute(x, 'pair', [(i, at[place[i], 1 - core[i]]) for i in range(le...  1.31 us
  transfers between devices with their start and end apart: 32, of which 13 were waited for; matrix products, arithmetic and copies ran while one was open for 2% of the time, Pallas kernels for 8%

profile of v1, /device:TPU:0, one launch (start us, length us, event | category | flops | bytes accessed | tf_op | source)
XLA Modules:
  0.0 58.5 jit_solution(17548959008231789272)
XLA Ops:
  0.0 0.8 %convert_reduce_fusion = s32[8]{0:T(128)S(1)} fusion(s32[512]{0:T(512)} %param.15), kind=kLoop, calls=%fused_computation | loop fusion | flops 12280 | bytes 2080 | tf_op jit(solution)/shard_map/reduce_sum | solution.py:304
  0.8 0.6 %reduce_max.9 = s32[]{:T(128)} reduce(s32[8]{0:T(128)S(1)} %convert_reduce_fusion, s32[]{:T(128)} %constant.3.clone.1), dimensions={0}, to_apply=%region_1.0 | reduce | flops 7 | bytes 40 | tf_op jit(solution)/shard_map/reduce_max | solution.py:304
  2.1 56.4 %conditional.1 = (bf16[5,256,512]{2,1,0:T(8,128)(2,1)}) conditional(s32[]{:T(128)} %convert_element_type.7, (s32[512]{0:T(512)}, bf16[3,256,512]{2,1,0:T(8,128)(2,1)}, s32[5,2]{0,1:T(2,128)}, s32[48]{0:T(128)}, bf16[5,256,512]{2,1,0:T(8,128)(2,1)}, /*index=5*/(), ()) %tuple.11, (s32[512]{0:T(512)}, bf16[3,256,512]{2,1,0:T(8,128)(2,1)}, ...), branch_computations={%region_2.0_spmd, %region_3.0_spmd} | conditional | flops 671088640 | bytes 210250720 | solution.py:313
  2.1 2.7 %compact_inter.3 = (bf16[3,96,256]{2,1,0:T(8,128)(2,1)}, bf16[96,512]{1,0:T(8,128)(2,1)}, bf16[96,256]{1,0:T(8,128)(2,1)}, bf16[8,256]{1,0:T(8,128)(2,1)}) custom-call(s32[1,512]{1,0:T(1,128)} %bitcast.5, bf16[3,256,512]{2,1,0:T(8,128)(2,1)} %get-tuple-element.74.inter_ref), custom_call_target="tpu_custom_call" | custom-call | tf_op jit(solution)/shard_map/cond/branch_1_fun/compact_inter/pallas_call | solution.py:286
  4.9 3.0 %collective-permute-start.47 = (bf16[3,96,256]{2,1,0:T(8,128)(2,1)}, bf16[3,96,256]{2,1,0:T(8,128)(2,1)S(1)}, u32[]{:S(2)}, u32[]{:S(2)}) collective-permute-start(bf16[3,96,256]{2,1,0:T(8,128)(2,1)} %get-tuple-element.57.refs_0_), channel_id=1, source_target_pairs={{1,0},{0,1},{3,2},{2,3},{5,4},{4,5},{7,6},{6,7},{9,8},{8,9},{11,10... | collective-permute-start | bytes 442376 | tf_op jit(solution)/shard_map/cond/branch_1_fun/ppermute | solution.py:205
  7.9 1.3 %copy.27.orbitals_ref = s32[5,2]{1,0:T(8,128)} copy(s32[5,2]{0,1:T(2,128)} %get-tuple-element.108) | data formatting | bytes 80 | tf_op jit(solution)/shard_map
  9.2 4.8 %compact_amp.3.refs_32_ = bf16[5,96,256]{2,1,0:T(8,128)(2,1)} custom-call(s32[5,2]{1,0:T(8,128)} %copy.27.orbitals_ref, s32[48]{0:T(128)} %get-tuple-element.78.occ_ref, s32[1,512]{1,0:T(1,128)} %bitcast.6, bf16[8,256]{1,0:T(8,128)(2,1)} %get-tuple-element.53.hot_own_ref, bf16[96,512]{1,0:T(8,128)(2,1)} %get-tuple-element.54.ranks_ref, ...), custom_call_target="tpu_custom_call" | custom-call | flops 125829120 | bytes 1556480 | tf_op jit(solution)/shard_map/cond/branch_1_fun/compact_amp/pallas_call | solution.py:219
  14.1 1.9 %collective-permute-start.36 = (bf16[3,96,256]{2,1,0:T(8,128)(2,1)S(1)}, bf16[3,96,256]{2,1,0:T(8,128)(2,1)S(1)}, u32[]{:S(2)}, u32[]{:S(2)}) collective-permute-start(bf16[3,96,256]{2,1,0:T(8,128)(2,1)S(1)} %copy-done.34), channel_id=1, source_target_pairs={{0,4},{2,6},{4,12},{6,14},{8,0},{10,2},{12,20},{14,22},{16,8},{18,... | collective-permute-start | bytes 442376 | tf_op jit(solution)/shard_map/cond/branch_1_fun/ppermute | solution.py:196
  16.2 2.0 %collective-permute-start.51 = (bf16[3,96,256]{2,1,0:T(8,128)(2,1)S(1)}, bf16[3,96,256]{2,1,0:T(8,128)(2,1)S(1)}, u32[]{:S(2)}, u32[]{:S(2)}) collective-permute-start(bf16[3,96,256]{2,1,0:T(8,128)(2,1)S(1)} %collective-permute-done.47.refs_16_), channel_id=1, source_target_pairs={{0,4},{2,6},{4,12},{6,14},{8,0},{10,2},{12,20},{14,22},{16,8},{18,... | collective-permute-start | bytes 442376 | tf_op jit(solution)/shard_map/cond/branch_1_fun/ppermute | solution.py:196
  18.2 2.7 %collective-permute-done.36.refs_7_ = bf16[3,96,256]{2,1,0:T(8,128)(2,1)S(1)} collective-permute-done((bf16[3,96,256]{2,1,0:T(8,128)(2,1)S(1)}, bf16[3,96,256]{2,1,0:T(8,128)(2,1)S(1)}, u32[]{:S(2)}, u32[]{:S(2)}) %collective-permute-start.36) | collective-permute-done | bytes 147488 | tf_op jit(solution)/shard_map/cond/branch_1_fun/ppermute | solution.py:196
  20.9 2.0 %collective-permute-start.48 = (bf16[3,96,256]{2,1,0:T(8,128)(2,1)S(1)}, bf16[3,96,256]{2,1,0:T(8,128)(2,1)S(1)}, u32[]{:S(2)}, u32[]{:S(2)}) collective-permute-start(bf16[3,96,256]{2,1,0:T(8,128)(2,1)S(1)} %collective-permute-done.47.refs_16_), channel_id=1, source_target_pairs={{0,8},{2,10},{4,0},{6,2},{8,16},{10,18},{12,4},{14,6},{16,24},{18,... | collective-permute-start | bytes 442376 | tf_op jit(solution)/shard_map/cond/branch_1_fun/ppermute | solution.py:196
  22.9 1.2 %collective-permute-start.37 = (bf16[3,96,256]{2,1,0:T(8,128)(2,1)S(1)}, bf16[3,96,256]{2,1,0:T(8,128)(2,1)S(1)}, u32[]{:S(2)}, u32[]{:S(2)}) collective-permute-start(bf16[3,96,256]{2,1,0:T(8,128)(2,1)S(1)} %collective-permute-done.36.refs_7_), channel_id=1, source_target_pairs={{0,4},{2,6},{4,12},{6,14},{8,0},{10,2},{12,20},{14,22},{16,8},{18,... | collective-permute-start | bytes 442376 | tf_op jit(solution)/shard_map/cond/branch_1_fun/ppermute | solution.py:196
  24.1 1.1 %collective-permute-start.33 = (bf16[3,96,256]{2,1,0:T(8,128)(2,1)S(1)}, bf16[3,96,256]{2,1,0:T(8,128)(2,1)S(1)}, u32[]{:S(2)}, u32[]{:S(2)}) collective-permute-start(bf16[3,96,256]{2,1,0:T(8,128)(2,1)S(1)} %collective-permute-done.32.refs_1_), channel_id=1, source_target_pairs={{0,8},{2,10},{4,0},{6,2},{8,16},{10,18},{12,4},{14,6},{16,24},{18,... | collective-permute-start | bytes 442376 | tf_op jit(solution)/shard_map/cond/branch_1_fun/ppermute | solution.py:196
  25.3 0.7 %collective-permute-done.48.refs_17_ = bf16[3,96,256]{2,1,0:T(8,128)(2,1)S(1)} collective-permute-done((bf16[3,96,256]{2,1,0:T(8,128)(2,1)S(1)}, bf16[3,96,256]{2,1,0:T(8,128)(2,1)S(1)}, u32[]{:S(2)}, u32[]{:S(2)}) %collective-permute-start.48) | collective-permute-done | bytes 147488 | tf_op jit(solution)/shard_map/cond/branch_1_fun/ppermute | solution.py:196
  26.0 2.0 %collective-permute-start.52 = (bf16[3,96,256]{2,1,0:T(8,128)(2,1)S(1)}, bf16[3,96,256]{2,1,0:T(8,128)(2,1)S(1)}, u32[]{:S(2)}, u32[]{:S(2)}) collective-permute-start(bf16[3,96,256]{2,1,0:T(8,128)(2,1)S(1)} %collective-permute-done.51.refs_23_), channel_id=1, source_target_pairs={{0,4},{2,6},{4,12},{6,14},{8,0},{10,2},{12,20},{14,22},{16,8},{18,... | collective-permute-start | bytes 442376 | tf_op jit(solution)/shard_map/cond/branch_1_fun/ppermute | solution.py:196
  28.0 1.1 %collective-permute-done.37.refs_6_ = bf16[3,96,256]{2,1,0:T(8,128)(2,1)S(1)} collective-permute-done((bf16[3,96,256]{2,1,0:T(8,128)(2,1)S(1)}, bf16[3,96,256]{2,1,0:T(8,128)(2,1)S(1)}, u32[]{:S(2)}, u32[]{:S(2)}) %collective-permute-start.37) | collective-permute-done | bytes 147488 | tf_op jit(solution)/shard_map/cond/branch_1_fun/ppermute | solution.py:196
  29.2 1.6 %collective-permute-start.49 = (bf16[3,96,256]{2,1,0:T(8,128)(2,1)S(1)}, bf16[3,96,256]{2,1,0:T(8,128)(2,1)S(1)}, u32[]{:S(2)}, u32[]{:S(2)}) collective-permute-start(bf16[3,96,256]{2,1,0:T(8,128)(2,1)S(1)} %collective-permute-done.48.refs_17_), channel_id=1, source_target_pairs={{0,8},{2,10},{4,0},{6,2},{8,16},{10,18},{12,4},{14,6},{16,24},{18,... | collective-permute-start | bytes 442376 | tf_op jit(solution)/shard_map/cond/branch_1_fun/ppermute | solution.py:196
  30.9 1.1 %collective-permute-start.38 = (bf16[3,96,256]{2,1,0:T(8,128)(2,1)S(1)}, bf16[3,96,256]{2,1,0:T(8,128)(2,1)S(1)}, u32[]{:S(2)}, u32[]{:S(2)}) collective-permute-start(bf16[3,96,256]{2,1,0:T(8,128)(2,1)S(1)} %collective-permute-done.37.refs_6_), channel_id=1, source_target_pairs={{0,4},{2,6},{4,12},{6,14},{8,0},{10,2},{12,20},{14,22},{16,8},{18,... | collective-permute-start | bytes 442376 | tf_op jit(solution)/shard_map/cond/branch_1_fun/ppermute | solution.py:196
  32.6 1.8 %collective-permute-start.34 = (bf16[3,96,256]{2,1,0:T(8,128)(2,1)S(1)}, bf16[3,96,256]{2,1,0:T(8,128)(2,1)S(1)}, u32[]{:S(2)}, u32[]{:S(2)}) collective-permute-start(bf16[3,96,256]{2,1,0:T(8,128)(2,1)S(1)} %collective-permute-done.33.refs_2_), channel_id=1, source_target_pairs={{0,8},{2,10},{4,0},{6,2},{8,16},{10,18},{12,4},{14,6},{16,24},{18,... | collective-permute-start | bytes 442376 | tf_op jit(solution)/shard_map/cond/branch_1_fun/ppermute | solution.py:196
  34.3 1.1 %collective-permute-done.49.refs_18_ = bf16[3,96,256]{2,1,0:T(8,128)(2,1)S(1)} collective-permute-done((bf16[3,96,256]{2,1,0:T(8,128)(2,1)S(1)}, bf16[3,96,256]{2,1,0:T(8,128)(2,1)S(1)}, u32[]{:S(2)}, u32[]{:S(2)}) %collective-permute-start.49) | collective-permute-done | bytes 147488 | tf_op jit(solution)/shard_map/cond/branch_1_fun/ppermute | solution.py:196
  35.9 1.1 %collective-permute-done.38.refs_5_ = bf16[3,96,256]{2,1,0:T(8,128)(2,1)S(1)} collective-permute-done((bf16[3,96,256]{2,1,0:T(8,128)(2,1)S(1)}, bf16[3,96,256]{2,1,0:T(8,128)(2,1)S(1)}, u32[]{:S(2)}, u32[]{:S(2)}) %collective-permute-start.38) | collective-permute-done | bytes 147488 | tf_op jit(solution)/shard_map/cond/branch_1_fun/ppermute | solution.py:196
  37.1 1.6 %collective-permute-start.50 = (bf16[3,96,256]{2,1,0:T(8,128)(2,1)S(1)}, bf16[3,96,256]{2,1,0:T(8,128)(2,1)S(1)}, u32[]{:S(2)}, u32[]{:S(2)}) collective-permute-start(bf16[3,96,256]{2,1,0:T(8,128)(2,1)S(1)} %collective-permute-done.49.refs_18_), channel_id=1, source_target_pairs={{0,8},{2,10},{4,0},{6,2},{8,16},{10,18},{12,4},{14,6},{16,24},{18,... | collective-permute-start | bytes 442376 | tf_op jit(solution)/shard_map/cond/branch_1_fun/ppermute | solution.py:196
  38.9 1.7 %collective-permute-start.35 = (bf16[3,96,256]{2,1,0:T(8,128)(2,1)S(1)}, bf16[3,96,256]{2,1,0:T(8,128)(2,1)S(1)}, u32[]{:S(2)}, u32[]{:S(2)}) collective-permute-start(bf16[3,96,256]{2,1,0:T(8,128)(2,1)S(1)} %collective-permute-done.34.refs_3_), channel_id=1, source_target_pairs={{0,8},{2,10},{4,0},{6,2},{8,16},{10,18},{12,4},{14,6},{16,24},{18,... | collective-permute-start | bytes 442376 | tf_op jit(solution)/shard_map/cond/branch_1_fun/ppermute | solution.py:196
  40.6 1.1 %collective-permute-done.53.refs_21_ = bf16[3,96,256]{2,1,0:T(8,128)(2,1)S(1)} collective-permute-done((bf16[3,96,256]{2,1,0:T(8,128)(2,1)S(1)}, bf16[3,96,256]{2,1,0:T(8,128)(2,1)S(1)}, u32[]{:S(2)}, u32[]{:S(2)}) %collective-permute-start.53) | collective-permute-done | bytes 147488 | tf_op jit(solution)/shard_map/cond/branch_1_fun/ppermute | solution.py:196
  42.2 1.6 %collective-permute-done.50.refs_19_ = bf16[3,96,256]{2,1,0:T(8,128)(2,1)S(1)} collective-permute-done((bf16[3,96,256]{2,1,0:T(8,128)(2,1)S(1)}, bf16[3,96,256]{2,1,0:T(8,128)(2,1)S(1)}, u32[]{:S(2)}, u32[]{:S(2)}) %collective-permute-start.50) | collective-permute-done | bytes 147488 | tf_op jit(solution)/shard_map/cond/branch_1_fun/ppermute | solution.py:196
  43.9 0.6 collective-permute-start.58
  44.4 2.0 %collective-permute-done.35.refs_4_ = bf16[3,96,256]{2,1,0:T(8,128)(2,1)S(1)} collective-permute-done((bf16[3,96,256]{2,1,0:T(8,128)(2,1)S(1)}, bf16[3,96,256]{2,1,0:T(8,128)(2,1)S(1)}, u32[]{:S(2)}, u32[]{:S(2)}) %collective-permute-start.35) | collective-permute-done | bytes 147488 | tf_op jit(solution)/shard_map/cond/branch_1_fun/ppermute | solution.py:196
  46.5 0.5 collective-permute-done.54.refs_20_
  47.1 0.7 %collective-permute-done.43.refs_12_ = bf16[3,96,256]{2,1,0:T(8,128)(2,1)S(1)} collective-permute-done((bf16[3,96,256]{2,1,0:T(8,128)(2,1)S(1)}, bf16[3,96,256]{2,1,0:T(8,128)(2,1)S(1)}, u32[]{:S(2)}, u32[]{:S(2)}) %collective-permute-start.43) | collective-permute-done | bytes 147488 | tf_op jit(solution)/shard_map/cond/branch_1_fun/ppermute | solution.py:201
  47.9 0.5 collective-permute-done.59.refs_28_
  48.5 0.7 %copy-done.65 = bf16[3,96,256]{2,1,0:T(8,128)(2,1)} copy-done((bf16[3,96,256]{2,1,0:T(8,128)(2,1)}, bf16[3,96,256]{2,1,0:T(8,128)(2,1)S(1)}, u32[]{:S(2)}) %copy-start.65) | copy-done | bytes 147480 | tf_op jit(solution)/shard_map/cond
  49.3 9.2 %residual.3 = bf16[5,256,512]{2,1,0:T(8,128)(2,1)} custom-call(s32[5,2]{1,0:T(8,128)} %copy.27.orbitals_ref, s32[48]{0:T(128)S(1)} %copy-done.69, s32[16]{0:T(128)} %constant.10.clone.2.place_ref, s32[16]{0:T(128)} %constant.11.clone.2.core_ref, s32[1,512]{1,0:T(1,128)S(1)} %bitcast.7, bf16[8,256]{1,0:T(8,128)(2,1)} %get-tuple-element.53.hot_own_ref, ...), custom_call_target="tpu_custom_call" | custom-call | tf_op jit(solution)/shard_map/cond/branch_1_fun/residual/pallas_call | solution.py:257
  (111 shorter events, 2.4 us)
Async XLA Ops:
  4.9 11.3 %collective-permute-start.47 = (bf16[3,96,256]{2,1,0:T(8,128)(2,1)}, bf16[3,96,256]{2,1,0:T(8,128)(2,1)S(1)}, u32[]{:S(2)}, u32[]{:S(2)}) collective-permute-start(bf16[3,96,256]{2,1,0:T(8,128)(2,1)} %get-tuple-element.57.refs_0_), channel_id=1, source_target_pairs={{1,0},{0,1},{3,2},{2,3},{5,4},{4,5},{7,6},{6,7},{9,8},{8,9},{11,10... | collective-permute-start | bytes 442376 | tf_op jit(solution)/shard_map/cond/branch_1_fun/ppermute | solution.py:205
  7.9 8.3 %collective-permute-start.39 = (bf16[3,96,256]{2,1,0:T(8,128)(2,1)}, bf16[3,96,256]{2,1,0:T(8,128)(2,1)S(1)}, u32[]{:S(2)}, u32[]{:S(2)}) collective-permute-start(bf16[3,96,256]{2,1,0:T(8,128)(2,1)} %get-tuple-element.57.refs_0_), channel_id=1, source_target_pairs={{0,2},{2,0},{4,6},{6,4},{8,10},{10,8},{12,14},{14,12},{16,18},{18,... | collective-permute-start | bytes 442376 | tf_op jit(solution)/shard_map/cond/branch_1_fun/ppermute | solution.py:201
  14.0 8.8 %collective-permute-start.63 = (bf16[5,96,256]{2,1,0:T(8,128)(2,1)}, bf16[5,96,256]{2,1,0:T(8,128)(2,1)S(1)}, u32[]{:S(2)}, u32[]{:S(2)}) collective-permute-start(bf16[5,96,256]{2,1,0:T(8,128)(2,1)} %compact_amp.3.refs_32_), channel_id=1, source_target_pairs={{1,0},{0,1},{3,2},{2,3},{5,4},{4,5},{7,6},{6,7},{9,8},{8,9},{11,10... | collective-permute-start | bytes 737288 | tf_op jit(solution)/shard_map/cond/branch_1_fun/ppermute | solution.py:205
  14.1 6.7 %collective-permute-start.36 = (bf16[3,96,256]{2,1,0:T(8,128)(2,1)S(1)}, bf16[3,96,256]{2,1,0:T(8,128)(2,1)S(1)}, u32[]{:S(2)}, u32[]{:S(2)}) collective-permute-start(bf16[3,96,256]{2,1,0:T(8,128)(2,1)S(1)} %copy-done.34), channel_id=1, source_target_pairs={{0,4},{2,6},{4,12},{6,14},{8,0},{10,2},{12,20},{14,22},{16,8},{18,... | collective-permute-start | bytes 442376 | tf_op jit(solution)/shard_map/cond/branch_1_fun/ppermute | solution.py:196
  16.0 6.8 %collective-permute-start.32 = (bf16[3,96,256]{2,1,0:T(8,128)(2,1)S(1)}, bf16[3,96,256]{2,1,0:T(8,128)(2,1)S(1)}, u32[]{:S(2)}, u32[]{:S(2)}) collective-permute-start(bf16[3,96,256]{2,1,0:T(8,128)(2,1)S(1)} %copy-done.34), channel_id=1, source_target_pairs={{0,8},{2,10},{4,0},{6,2},{8,16},{10,18},{12,4},{14,6},{16,24},{18,... | collective-permute-start | bytes 442376 | tf_op jit(solution)/shard_map/cond/branch_1_fun/ppermute | solution.py:196
  16.2 8.0 %collective-permute-start.55 = (bf16[3,96,256]{2,1,0:T(8,128)(2,1)S(1)}, bf16[3,96,256]{2,1,0:T(8,128)(2,1)S(1)}, u32[]{:S(2)}, u32[]{:S(2)}) collective-permute-start(bf16[3,96,256]{2,1,0:T(8,128)(2,1)S(1)} %collective-permute-done.47.refs_16_), channel_id=1, source_target_pairs={{0,2},{2,0},{4,6},{6,4},{8,10},{10,8},{12,14},{14,12},{16,18},{18,... | collective-permute-start | bytes 442376 | tf_op jit(solution)/shard_map/cond/branch_1_fun/ppermute | solution.py:201
  16.2 7.9 %collective-permute-start.51 = (bf16[3,96,256]{2,1,0:T(8,128)(2,1)S(1)}, bf16[3,96,256]{2,1,0:T(8,128)(2,1)S(1)}, u32[]{:S(2)}, u32[]{:S(2)}) collective-permute-start(bf16[3,96,256]{2,1,0:T(8,128)(2,1)S(1)} %collective-permute-done.47.refs_16_), channel_id=1, source_target_pairs={{0,4},{2,6},{4,12},{6,14},{8,0},{10,2},{12,20},{14,22},{16,8},{18,... | collective-permute-start | bytes 442376 | tf_op jit(solution)/shard_map/cond/branch_1_fun/ppermute | solution.py:196
  20.9 5.1 %collective-permute-start.48 = (bf16[3,96,256]{2,1,0:T(8,128)(2,1)S(1)}, bf16[3,96,256]{2,1,0:T(8,128)(2,1)S(1)}, u32[]{:S(2)}, u32[]{:S(2)}) collective-permute-start(bf16[3,96,256]{2,1,0:T(8,128)(2,1)S(1)} %collective-permute-done.47.refs_16_), channel_id=1, source_target_pairs={{0,8},{2,10},{4,0},{6,2},{8,16},{10,18},{12,4},{14,6},{16,24},{18,... | collective-permute-start | bytes 442376 | tf_op jit(solution)/shard_map/cond/branch_1_fun/ppermute | solution.py:196
  22.9 3.1 %collective-permute-start.46 = (bf16[3,96,256]{2,1,0:T(8,128)(2,1)S(1)}, bf16[3,96,256]{2,1,0:T(8,128)(2,1)S(1)}, u32[]{:S(2)}, u32[]{:S(2)}) collective-permute-start(bf16[3,96,256]{2,1,0:T(8,128)(2,1)S(1)} %collective-permute-done.36.refs_7_), channel_id=1, source_target_pairs={{0,2},{2,0},{4,6},{6,4},{8,10},{10,8},{12,14},{14,12},{16,18},{18,... | collective-permute-start | bytes 442376 | tf_op jit(solution)/shard_map/cond/branch_1_fun/ppermute | solution.py:201
  22.9 6.2 %collective-permute-start.37 = (bf16[3,96,256]{2,1,0:T(8,128)(2,1)S(1)}, bf16[3,96,256]{2,1,0:T(8,128)(2,1)S(1)}, u32[]{:S(2)}, u32[]{:S(2)}) collective-permute-start(bf16[3,96,256]{2,1,0:T(8,128)(2,1)S(1)} %collective-permute-done.36.refs_7_), channel_id=1, source_target_pairs={{0,4},{2,6},{4,12},{6,14},{8,0},{10,2},{12,20},{14,22},{16,8},{18,... | collective-permute-start | bytes 442376 | tf_op jit(solution)/shard_map/cond/branch_1_fun/ppermute | solution.py:196
  24.1 5.0 %collective-permute-start.40 = (bf16[3,96,256]{2,1,0:T(8,128)(2,1)S(1)}, bf16[3,96,256]{2,1,0:T(8,128)(2,1)S(1)}, u32[]{:S(2)}, u32[]{:S(2)}) collective-permute-start(bf16[3,96,256]{2,1,0:T(8,128)(2,1)S(1)} %collective-permute-done.32.refs_1_), channel_id=1, source_target_pairs={{0,2},{2,0},{4,6},{6,4},{8,10},{10,8},{12,14},{14,12},{16,18},{18,... | collective-permute-start | bytes 442376 | tf_op jit(solution)/shard_map/cond/branch_1_fun/ppermute | solution.py:201
  24.1 6.6 %collective-permute-start.33 = (bf16[3,96,256]{2,1,0:T(8,128)(2,1)S(1)}, bf16[3,96,256]{2,1,0:T(8,128)(2,1)S(1)}, u32[]{:S(2)}, u32[]{:S(2)}) collective-permute-start(bf16[3,96,256]{2,1,0:T(8,128)(2,1)S(1)} %collective-permute-done.32.refs_1_), channel_id=1, source_target_pairs={{0,8},{2,10},{4,0},{6,2},{8,16},{10,18},{12,4},{14,6},{16,24},{18,... | collective-permute-start | bytes 442376 | tf_op jit(solution)/shard_map/cond/branch_1_fun/ppermute | solution.py:196
  26.0 4.9 %collective-permute-start.62 = (bf16[3,96,256]{2,1,0:T(8,128)(2,1)S(1)}, bf16[3,96,256]{2,1,0:T(8,128)(2,1)S(1)}, u32[]{:S(2)}, u32[]{:S(2)}) collective-permute-start(bf16[3,96,256]{2,1,0:T(8,128)(2,1)S(1)} %collective-permute-done.51.refs_23_), channel_id=1, source_target_pairs={{0,2},{2,0},{4,6},{6,4},{8,10},{10,8},{12,14},{14,12},{16,18},{18,... | collective-permute-start | bytes 442376 | tf_op jit(solution)/shard_map/cond/branch_1_fun/ppermute | solution.py:201
  26.0 6.5 %collective-permute-start.52 = (bf16[3,96,256]{2,1,0:T(8,128)(2,1)S(1)}, bf16[3,96,256]{2,1,0:T(8,128)(2,1)S(1)}, u32[]{:S(2)}, u32[]{:S(2)}) collective-permute-start(bf16[3,96,256]{2,1,0:T(8,128)(2,1)S(1)} %collective-permute-done.51.refs_23_), channel_id=1, source_target_pairs={{0,4},{2,6},{4,12},{6,14},{8,0},{10,2},{12,20},{14,22},{16,8},{18,... | collective-permute-start | bytes 442376 | tf_op jit(solution)/shard_map/cond/branch_1_fun/ppermute | solution.py:196
  29.1 3.4 %collective-permute-start.56 = (bf16[3,96,256]{2,1,0:T(8,128)(2,1)S(1)}, bf16[3,96,256]{2,1,0:T(8,128)(2,1)S(1)}, u32[]{:S(2)}, u32[]{:S(2)}) collective-permute-start(bf16[3,96,256]{2,1,0:T(8,128)(2,1)S(1)} %collective-permute-done.48.refs_17_), channel_id=1, source_target_pairs={{0,2},{2,0},{4,6},{6,4},{8,10},{10,8},{12,14},{14,12},{16,18},{18,... | collective-permute-start | bytes 442376 | tf_op jit(solution)/shard_map/cond/branch_1_fun/ppermute | solution.py:201
  29.2 6.3 %collective-permute-start.49 = (bf16[3,96,256]{2,1,0:T(8,128)(2,1)S(1)}, bf16[3,96,256]{2,1,0:T(8,128)(2,1)S(1)}, u32[]{:S(2)}, u32[]{:S(2)}) collective-permute-start(bf16[3,96,256]{2,1,0:T(8,128)(2,1)S(1)} %collective-permute-done.48.refs_17_), channel_id=1, source_target_pairs={{0,8},{2,10},{4,0},{6,2},{8,16},{10,18},{12,4},{14,6},{16,24},{18,... | collective-permute-start | bytes 442376 | tf_op jit(solution)/shard_map/cond/branch_1_fun/ppermute | solution.py:196
  30.8 4.6 %collective-permute-start.45 = (bf16[3,96,256]{2,1,0:T(8,128)(2,1)S(1)}, bf16[3,96,256]{2,1,0:T(8,128)(2,1)S(1)}, u32[]{:S(2)}, u32[]{:S(2)}) collective-permute-start(bf16[3,96,256]{2,1,0:T(8,128)(2,1)S(1)} %collective-permute-done.37.refs_6_), channel_id=1, source_target_pairs={{0,2},{2,0},{4,6},{6,4},{8,10},{10,8},{12,14},{14,12},{16,18},{18,... | collective-permute-start | bytes 442376 | tf_op jit(solution)/shard_map/cond/branch_1_fun/ppermute | solution.py:201
  30.9 6.1 %collective-permute-start.38 = (bf16[3,96,256]{2,1,0:T(8,128)(2,1)S(1)}, bf16[3,96,256]{2,1,0:T(8,128)(2,1)S(1)}, u32[]{:S(2)}, u32[]{:S(2)}) collective-permute-start(bf16[3,96,256]{2,1,0:T(8,128)(2,1)S(1)} %collective-permute-done.37.refs_6_), channel_id=1, source_target_pairs={{0,4},{2,6},{4,12},{6,14},{8,0},{10,2},{12,20},{14,22},{16,8},{18,... | collective-permute-start | bytes 442376 | tf_op jit(solution)/shard_map/cond/branch_1_fun/ppermute | solution.py:196
  32.5 4.5 %collective-permute-start.41 = (bf16[3,96,256]{2,1,0:T(8,128)(2,1)S(1)}, bf16[3,96,256]{2,1,0:T(8,128)(2,1)S(1)}, u32[]{:S(2)}, u32[]{:S(2)}) collective-permute-start(bf16[3,96,256]{2,1,0:T(8,128)(2,1)S(1)} %collective-permute-done.33.refs_2_), channel_id=1, source_target_pairs={{0,2},{2,0},{4,6},{6,4},{8,10},{10,8},{12,14},{14,12},{16,18},{18,... | collective-permute-start | bytes 442376 | tf_op jit(solution)/shard_map/cond/branch_1_fun/ppermute | solution.py:201
  32.6 6.3 %collective-permute-start.34 = (bf16[3,96,256]{2,1,0:T(8,128)(2,1)S(1)}, bf16[3,96,256]{2,1,0:T(8,128)(2,1)S(1)}, u32[]{:S(2)}, u32[]{:S(2)}) collective-permute-start(bf16[3,96,256]{2,1,0:T(8,128)(2,1)S(1)} %collective-permute-done.33.refs_2_), channel_id=1, source_target_pairs={{0,8},{2,10},{4,0},{6,2},{8,16},{10,18},{12,4},{14,6},{16,24},{18,... | collective-permute-start | bytes 442376 | tf_op jit(solution)/shard_map/cond/branch_1_fun/ppermute | solution.py:196
  35.4 3.5 %collective-permute-start.61 = (bf16[3,96,256]{2,1,0:T(8,128)(2,1)S(1)}, bf16[3,96,256]{2,1,0:T(8,128)(2,1)S(1)}, u32[]{:S(2)}, u32[]{:S(2)}) collective-permute-start(bf16[3,96,256]{2,1,0:T(8,128)(2,1)S(1)} %collective-permute-done.52.refs_22_), channel_id=1, source_target_pairs={{0,2},{2,0},{4,6},{6,4},{8,10},{10,8},{12,14},{14,12},{16,18},{18,... | collective-permute-start | bytes 442376 | tf_op jit(solution)/shard_map/cond/branch_1_fun/ppermute | solution.py:201
  35.4 6.3 %collective-permute-start.53 = (bf16[3,96,256]{2,1,0:T(8,128)(2,1)S(1)}, bf16[3,96,256]{2,1,0:T(8,128)(2,1)S(1)}, u32[]{:S(2)}, u32[]{:S(2)}) collective-permute-start(bf16[3,96,256]{2,1,0:T(8,128)(2,1)S(1)} %collective-permute-done.52.refs_22_), channel_id=1, source_target_pairs={{0,4},{2,6},{4,12},{6,14},{8,0},{10,2},{12,20},{14,22},{16,8},{18,... | collective-permute-start | bytes 442376 | tf_op jit(solution)/shard_map/cond/branch_1_fun/ppermute | solution.py:196
  37.1 5.1 %collective-permute-start.57 = (bf16[3,96,256]{2,1,0:T(8,128)(2,1)S(1)}, bf16[3,96,256]{2,1,0:T(8,128)(2,1)S(1)}, u32[]{:S(2)}, u32[]{:S(2)}) collective-permute-start(bf16[3,96,256]{2,1,0:T(8,128)(2,1)S(1)} %collective-permute-done.49.refs_18_), channel_id=1, source_target_pairs={{0,2},{2,0},{4,6},{6,4},{8,10},{10,8},{12,14},{14,12},{16,18},{18,... | collective-permute-start | bytes 442376 | tf_op jit(solution)/shard_map/cond/branch_1_fun/ppermute | solution.py:201
  37.1 6.8 %collective-permute-start.50 = (bf16[3,96,256]{2,1,0:T(8,128)(2,1)S(1)}, bf16[3,96,256]{2,1,0:T(8,128)(2,1)S(1)}, u32[]{:S(2)}, u32[]{:S(2)}) collective-permute-start(bf16[3,96,256]{2,1,0:T(8,128)(2,1)S(1)} %collective-permute-done.49.refs_18_), channel_id=1, source_target_pairs={{0,8},{2,10},{4,0},{6,2},{8,16},{10,18},{12,4},{14,6},{16,24},{18,... | collective-permute-start | bytes 442376 | tf_op jit(solution)/shard_map/cond/branch_1_fun/ppermute | solution.py:196
  38.8 5.1 %collective-permute-start.44 = (bf16[3,96,256]{2,1,0:T(8,128)(2,1)S(1)}, bf16[3,96,256]{2,1,0:T(8,128)(2,1)S(1)}, u32[]{:S(2)}, u32[]{:S(2)}) collective-permute-start(bf16[3,96,256]{2,1,0:T(8,128)(2,1)S(1)} %collective-permute-done.38.refs_5_), channel_id=1, source_target_pairs={{0,2},{2,0},{4,6},{6,4},{8,10},{10,8},{12,14},{14,12},{16,18},{18,... | collective-permute-start | bytes 442376 | tf_op jit(solution)/shard_map/cond/branch_1_fun/ppermute | solution.py:201
  38.9 7.6 %collective-permute-start.35 = (bf16[3,96,256]{2,1,0:T(8,128)(2,1)S(1)}, bf16[3,96,256]{2,1,0:T(8,128)(2,1)S(1)}, u32[]{:S(2)}, u32[]{:S(2)}) collective-permute-start(bf16[3,96,256]{2,1,0:T(8,128)(2,1)S(1)} %collective-permute-done.34.refs_3_), channel_id=1, source_target_pairs={{0,8},{2,10},{4,0},{6,2},{8,16},{10,18},{12,4},{14,6},{16,24},{18,... | collective-permute-start | bytes 442376 | tf_op jit(solution)/shard_map/cond/branch_1_fun/ppermute | solution.py:196
  41.7 5.3 %collective-permute-start.54 = (bf16[3,96,256]{2,1,0:T(8,128)(2,1)S(1)}, bf16[3,96,256]{2,1,0:T(8,128)(2,1)S(1)}, u32[]{:S(2)}, u32[]{:S(2)}) collective-permute-start(bf16[3,96,256]{2,1,0:T(8,128)(2,1)S(1)} %collective-permute-done.53.refs_21_), channel_id=1, source_target_pairs={{0,4},{2,6},{4,12},{6,14},{8,0},{10,2},{12,20},{14,22},{16,8},{18,... | collective-permute-start | bytes 442376 | tf_op jit(solution)/shard_map/cond/branch_1_fun/ppermute | solution.py:196
  42.2 4.9 %collective-permute-start.42 = (bf16[3,96,256]{2,1,0:T(8,128)(2,1)S(1)}, bf16[3,96,256]{2,1,0:T(8,128)(2,1)S(1)}, u32[]{:S(2)}, u32[]{:S(2)}) collective-permute-start(bf16[3,96,256]{2,1,0:T(8,128)(2,1)S(1)} %collective-permute-done.34.refs_3_), channel_id=1, source_target_pairs={{0,2},{2,0},{4,6},{6,4},{8,10},{10,8},{12,14},{14,12},{16,18},{18,... | collective-permute-start | bytes 442376 | tf_op jit(solution)/shard_map/cond/branch_1_fun/ppermute | solution.py:201
  43.8 3.2 %collective-permute-start.60 = (bf16[3,96,256]{2,1,0:T(8,128)(2,1)S(1)}, bf16[3,96,256]{2,1,0:T(8,128)(2,1)S(1)}, u32[]{:S(2)}, u32[]{:S(2)}) collective-permute-start(bf16[3,96,256]{2,1,0:T(8,128)(2,1)S(1)} %collective-permute-done.53.refs_21_), channel_id=1, source_target_pairs={{0,2},{2,0},{4,6},{6,4},{8,10},{10,8},{12,14},{14,12},{16,18},{18,... | collective-permute-start | bytes 442376 | tf_op jit(solution)/shard_map/cond/branch_1_fun/ppermute | solution.py:201
  43.9 3.2 %collective-permute-start.58 = (bf16[3,96,256]{2,1,0:T(8,128)(2,1)S(1)}, bf16[3,96,256]{2,1,0:T(8,128)(2,1)S(1)}, u32[]{:S(2)}, u32[]{:S(2)}) collective-permute-start(bf16[3,96,256]{2,1,0:T(8,128)(2,1)S(1)} %collective-permute-done.50.refs_19_), channel_id=1, source_target_pairs={{0,2},{2,0},{4,6},{6,4},{8,10},{10,8},{12,14},{14,12},{16,18},{18,... | collective-permute-start | bytes 442376 | tf_op jit(solution)/shard_map/cond/branch_1_fun/ppermute | solution.py:201
  46.5 1.4 %collective-permute-start.43 = (bf16[3,96,256]{2,1,0:T(8,128)(2,1)S(1)}, bf16[3,96,256]{2,1,0:T(8,128)(2,1)S(1)}, u32[]{:S(2)}, u32[]{:S(2)}) collective-permute-start(bf16[3,96,256]{2,1,0:T(8,128)(2,1)S(1)} %collective-permute-done.35.refs_4_), channel_id=1, source_target_pairs={{0,2},{2,0},{4,6},{6,4},{8,10},{10,8},{12,14},{14,12},{16,18},{18,... | collective-permute-start | bytes 442376 | tf_op jit(solution)/shard_map/cond/branch_1_fun/ppermute | solution.py:201
  47.0 1.4 %collective-permute-start.59 = (bf16[3,96,256]{2,1,0:T(8,128)(2,1)S(1)}, bf16[3,96,256]{2,1,0:T(8,128)(2,1)S(1)}, u32[]{:S(2)}, u32[]{:S(2)}) collective-permute-start(bf16[3,96,256]{2,1,0:T(8,128)(2,1)S(1)} %collective-permute-done.54.refs_20_), channel_id=1, source_target_pairs={{0,2},{2,0},{4,6},{6,4},{8,10},{10,8},{12,14},{14,12},{16,18},{18,... | collective-permute-start | bytes 442376 | tf_op jit(solution)/shard_map/cond/branch_1_fun/ppermute | solution.py:201
  (36 other events, 567.4 us)
